TPU v7x, 32 devices: a whole 2x2x4 slice. The times are simulated.
32 devices in a mesh: ax: 8 (over z, y), rad: 4 (over x, core).
Axes of the slice: x: 2, y: 2, z: 4, core: 2. Of those that a mesh axis runs over, the one named last changes fastest.
Arguments:
- face_data: float32 [1024, 7, 5, 128], P('ax', None, None, 'rad'), may hold values from -0.6 to 0.6
- face_station: int32 [1024], P('ax'), may hold values from 0 to 511, as said below
- face_counts: int32 [8], P('ax'), may hold values from 0 to 128, as said below
- mode_slots: int32 [256], replicated, may hold values from 0 to 255, each once
- radial_proj: float32 [32, 128], P(None, 'rad'), may hold values from -0.5 to 0.5
- radial_modes: float32 [64, 32], replicated, may hold values from -1 to 1
- duct_field: float32 [32, 64, 3, 5, 2, 256], P('ax', 'rad'), may hold values from -6 to 6
- mean_mach: float32 [32, 64], P('ax', 'rad'), may hold values from 0.1 to 0.7
- pseudo_step: float32 [32, 64], P('ax', 'rad'), may hold values from 0.06 to 0.2
Outputs:
- duct_next: float32 [32, 64, 3, 5, 2, 256], P('ax', 'rad')
Inputs may be any that keep to these rules, and one draw needn't show every extreme that they name: `face_counts`: they sum to 512; one index of ax uses all 128 slots. `face_station`: slot s of ax index a is used when s < face_counts[a] and then names an angular station; each station is named by exactly one used slot; unused slots name arbitrary stations. `mode_slots`: each circumferential mode once.
All inputs are finite; a program needn't handle non-finite values.
Results may differ from a plain program's by a relative error of at most 0.00012.
Values sent between devices are 32-bit elements; how exact they have to be, the bound alone decides.
A program may use at most 128 MiB of HBM per device.

v0:
```python
import math
import jax
import jax.numpy as jnp
from jax import lax
from jax.sharding import PartitionSpec as P

NTH = 512
SAMPLE_MOMENTS = 7
HARM = 3
NMODE = 256
NRD = 64
ITERS = 3
OMEGA_STEP = 0.35
DAMPING = 0.25


def extended(cells, sides, width):
    for axis, dim in sides:
        count = lax.axis_size(axis)
        ends = count - 1
        head = lax.slice_in_dim(cells, 0, width, axis=dim)
        tail = lax.slice_in_dim(cells, cells.shape[dim] - width, cells.shape[dim], axis=dim)
        cells = jnp.concatenate(
            [
                lax.ppermute(tail, axis, [(i, (i + 1) % count) for i in range(ends)]),
                cells,
                lax.ppermute(head, axis, [((i + 1) % count, i) for i in range(ends)]),
            ],
            axis=dim,
        )
    return cells


def rotate(part):
    return jnp.stack([-part[..., 1, :], part[..., 0, :]], axis=-2)


def advance(padded, mach, step_size, inv_radius, modes):
    centre = padded[1:-1, 1:-1]
    along = (padded[2:, 1:-1] - padded[:-2, 1:-1]) * 0.5
    across = (padded[1:-1, 2:] - padded[1:-1, :-2]) * 0.5
    damped_filter = (
        padded[2:, 1:-1] + padded[:-2, 1:-1] + padded[1:-1, 2:] + padded[1:-1, :-2] - 4.0 * centre
    )
    frequency_order = jnp.arange(1, HARM + 1).astype(jnp.float32)
    omega = (OMEGA_STEP * frequency_order)[:, None, None]
    mach_cell = mach[:, :, None, None, None]
    radius_cell = inv_radius[None, :, None, None, None]
    density = centre[:, :, :, 0]
    axial = centre[:, :, :, 1]
    radial = centre[:, :, :, 2]
    swirl = centre[:, :, :, 3]
    pressure = centre[:, :, :, 4]
    source = (
        along[:, :, :, 1]
        + across[:, :, :, 2]
        + radial * radius_cell
        + rotate(swirl) * modes * radius_cell
    )
    res_density = omega * rotate(density) + mach_cell * along[:, :, :, 0] + source
    res_axial = omega * rotate(axial) + mach_cell * along[:, :, :, 1] + along[:, :, :, 4]
    res_radial = omega * rotate(radial) + mach_cell * along[:, :, :, 2] + across[:, :, :, 4]
    res_swirl = (
        omega * rotate(swirl)
        + mach_cell * along[:, :, :, 3]
        + rotate(pressure) * modes * radius_cell
    )
    res_pressure = omega * rotate(pressure) + mach_cell * along[:, :, :, 4] + source
    residual = jnp.stack([res_density, res_axial, res_radial, res_swirl, res_pressure], axis=3)
    step_cell = step_size[:, :, None, None, None, None]
    return centre - step_cell * (residual - DAMPING * damped_filter)


def project(face_data, face_station, valid, wave_orders, radial_proj):
    frequency_order = jnp.arange(1, HARM + 1)
    sample_moments = jnp.arange(SAMPLE_MOMENTS)
    revolution_count = (frequency_order[:, None] * sample_moments[None, :] % SAMPLE_MOMENTS).astype(
        jnp.float32
    ) * (2.0 * math.pi / SAMPLE_MOMENTS)
    twiddle = jnp.stack([jnp.cos(revolution_count), -jnp.sin(revolution_count)], axis=1) * (
        2.0 / SAMPLE_MOMENTS
    )
    spectral_values = jnp.einsum(
        "rtvj,kct->rkvcj", face_data, twiddle, precision=lax.Precision.HIGHEST
    )
    phase = jnp.mod(face_station[:, None] * wave_orders[None, :], NTH).astype(jnp.float32) * (
        2.0 * math.pi / NTH
    )
    cosine = jnp.where(valid[:, None], jnp.cos(phase), 0.0)
    sine = jnp.where(valid[:, None], jnp.sin(phase), 0.0)
    with_cos = jnp.einsum(
        "rs,rkvcj->kvcjs", cosine, spectral_values, precision=lax.Precision.HIGHEST
    )
    with_sin = jnp.einsum("rs,rkvcj->kvcjs", sine, spectral_values, precision=lax.Precision.HIGHEST)
    real_part = with_cos[:, :, 0] + with_sin[:, :, 1]
    imag_part = with_cos[:, :, 1] - with_sin[:, :, 0]
    fourier_transform = jnp.stack([real_part, imag_part], axis=2)
    return jnp.einsum(
        "nj,kvcjs->nkvcs", radial_proj, fourier_transform, precision=lax.Precision.HIGHEST
    )


def on_device(
    face_data,
    face_station,
    face_counts,
    mode_slots,
    radial_proj,
    radial_modes,
    duct_field,
    mean_mach,
    pseudo_step,
):
    slot_ids = jnp.arange(face_station.shape[0])
    valid = slot_ids < face_counts[0]
    wave_orders = mode_slots - NMODE // 2
    partial_value = project(face_data, face_station, valid, wave_orders, radial_proj)
    rows_here = duct_field.shape[1]
    radial_index = lax.axis_index("rad")
    totals = lax.psum(partial_value, ("ax", "rad"))
    shape_rows = lax.dynamic_slice_in_dim(radial_modes, radial_index * rows_here, rows_here, 0)
    boundary = jnp.einsum("jn,nkvcs->jkvcs", shape_rows, totals, precision=lax.Precision.HIGHEST)
    modes = wave_orders.astype(jnp.float32)
    radial_start = radial_index * rows_here
    global_rows = (radial_start + jnp.arange(rows_here)).astype(jnp.float32)
    inv_radius = 1.0 / (NRD + global_rows + 0.5)
    at_inlet = lax.axis_index("ax") == 0
    field = duct_field
    for sweep in range(ITERS):
        padded = extended(field, (("ax", 0), ("rad", 1)), 1)
        ghost = jnp.where(at_inlet, boundary, padded[0, 1:-1])
        padded = padded.at[0, 1:-1].set(ghost)
        field = advance(padded, mean_mach, pseudo_step, inv_radius, modes)
    return field


def solution(mesh):
    in_specs = (
        P("ax", None, None, "rad"),
        P("ax"),
        P("ax"),
        P(),
        P(None, "rad"),
        P(),
        P("ax", "rad", None, None, None, None),
        P("ax", "rad"),
        P("ax", "rad"),
    )
    out_specs = P("ax", "rad", None, None, None, None)
    return jax.shard_map(
        on_device, mesh=mesh, in_specs=in_specs, out_specs=out_specs, check_vma=False
    )
```

profile of v0, /device:TPU:9, one launch (start us, length us, event | category | flops | bytes accessed | tf_op | source)
XLA Modules:
  0.0 296.3 jit_solution(11995770886220923457)
XLA Ops:
  6.5 1.2 slice.457
  7.8 3.3 %collective-permute-start = (f32[1,16,3,5,2,256]{5,1,2,4,3,0:T(8,128)S(1)}, f32[1,16,3,5,2,256]{5,1,2,4,3,0:T(8,128)S(1)}, u32[]{:S(2)}, u32[]{:S(2)}) collective-permute-start(f32[1,16,3,5,2,256]{5,1,2,4,3,0:T(8,128)S(1)} %copy.42), channel_id=1, source_target_pairs={{0,4},{4,8},{8,12},{12,16},{16,20},{20,24},{24,28},{1,5},{5,9},{9,... | collective-permute-start | bytes 1474568 | tf_op jit(solution)/shard_map/ppermute | solution.py:25
  11.1 1.8 copy.13
  13.0 0.8 slice.556
  13.8 3.0 %collective-permute-start.1 = (f32[1,16,3,5,2,256]{5,1,2,0,4,3:T(8,128)}, f32[1,16,3,5,2,256]{5,1,2,0,4,3:T(8,128)S(1)}, u32[]{:S(2)}, u32[]{:S(2)}) collective-permute-start(f32[1,16,3,5,2,256]{5,1,2,0,4,3:T(8,128)} %slice.556), channel_id=1, source_target_pairs={{4,0},{8,4},{12,8},{16,12},{20,16},{24,20},{28,24},{5,1},{9,5},{13... | collective-permute-start | bytes 1474568 | tf_op jit(solution)/shard_map/ppermute | solution.py:27
  17.7 1.2 convolution_bitcast_fusion.1
  18.9 1.5 fusion.47
  20.4 1.5 fusion.49
  21.9 0.2 slice_add_fusion
  22.1 1.9 convolution_bitcast_fusion
  24.0 0.7 fusion.118
  24.7 7.5 %collective-permute-done = f32[1,16,3,5,2,256]{5,1,2,4,3,0:T(8,128)S(1)} collective-permute-done((f32[1,16,3,5,2,256]{5,1,2,4,3,0:T(8,128)S(1)}, f32[1,16,3,5,2,256]{5,1,2,4,3,0:T(8,128)S(1)}, u32[]{:S(2)}, u32[]{:S(2)}) %collective-permute-start) | collective-permute-done | bytes 491552 | tf_op jit(solution)/shard_map/ppermute | solution.py:25
  32.2 2.9 collective-permute-done.1
  35.1 1.0 pad_maximum_fusion.17
  36.2 3.5 %collective-permute-start.2 = (f32[6,1,3,5,2,256]{5,1,2,0,4,3:T(1,128)}, f32[6,1,3,5,2,256]{5,1,2,0,4,3:T(1,128)}, u32[]{:S(2)}, u32[]{:S(2)}) collective-permute-start(f32[6,1,3,5,2,256]{5,1,2,0,4,3:T(1,128)} %get-tuple-element.76), channel_id=1, source_target_pairs={{0,1},{1,2},{2,3},{4,5},{5,6},{6,7},{8,9},{9,10},{10,11},{12,13},{... | collective-permute-start | bytes 552968 | tf_op jit(solution)/shard_map/ppermute | solution.py:25
  39.7 1.9 collective-permute-start.3
  41.6 112.0 %all-reduce.2.cloned.1.call-done = f32[32,3,5,2,256]{4,0,3,2,1:T(8,128)} async-done(((f32[32,3,5,2,256]{4,0,3,2,1:T(8,128)}), f32[32,3,5,2,256]{4,0,3,2,1:T(8,128)}) %all-reduce.2.cloned.1.call-update) | async-done | bytes 983056 | tf_op jit(solution)/shard_map/psum | solution.py:120
  153.6 1.9 fusion.82
  155.5 0.9 fusion.7
  156.3 3.8 %pad_maximum_fusion = f32[6,18,3,5,2,256]{5,1,2,0,4,3:T(8,128)} fusion(f32[6,1,3,5,2,256]{5,1,2,0,4,3:T(1,128)} %collective-permute-done.3, f32[1,16,3,5,2,256]{5,1,2,0,4,3:T(8,128)S(1)} %collective-permute-done.1, f32[4,16,3,5,2,256]{5,1,2,0,4,3:T(8,128)S(1)} %copy.13, f32[1,16,3,5,2,256]{5,1,2,0,4,3:T(8,128)S(1)} %bitcast.166, ...), kind=kLoop, calls=%fused_computation | loop fusion | flops 3317760 | bytes 6635520 | tf_op jit(solution)/shard_map/concatenate | solution.py:23
  160.2 5.0 %scatter.10 = f32[6,18,3,5,2,256]{5,1,2,0,4,3:T(8,128)} dynamic-update-slice(f32[6,18,3,5,2,256]{5,1,2,0,4,3:T(8,128)} %pad_maximum_fusion, f32[1,16,3,5,2,256]{5,1,2,0,4,3:T(8,128)} %fusion.7, s32[]{:T(128)} %bitcast.17, s32[]{:T(128)} %bitcast.18, s32[]{:T(128)} %constant.117.clone.1, s32[]{:T(128)} %constant.117.clone.1, s32[]{:T(128)} %constant.117.clone.1, s32[]{:T(128)} %constant.117.clone.1) | dynamic-update-slice | bytes 983044 | tf_op jit(solution)/shard_map/scatter | solution.py:132
  165.2 2.3 slice_bitcast_fusion.6
  167.5 5.5 %subtract_multiply_fusion.5 = (f32[4,16,3,5,2,256]{5,1,2,0,4,3:T(8,128)S(1)}, f32[4,16,3,5,2,256]{5,1,2,0,4,3:T(8,128)S(1)}) fusion(f32[6,18,3,5,2,256]{5,1,2,0,4,3:T(8,128)} %scatter.10), kind=kLoop, calls=%fused_computation.11 | loop fusion | flops 1966080 | bytes 11796480 | tf_op jit(solution)/shard_map/mul | solution.py:41
  173.2 0.4 copy-done.8
  173.6 0.3 fusion.37
  174.6 0.4 copy-done.9
  174.9 1.0 multiply_subtract_fusion.1
  176.0 3.2 %collective-permute-start.4 = (f32[1,16,3,5,2,256]{5,1,2,4,3,0:T(8,128)S(1)}, f32[1,16,3,5,2,256]{5,1,2,4,3,0:T(8,128)S(1)}, u32[]{:S(2)}, u32[]{:S(2)}) collective-permute-start(f32[1,16,3,5,2,256]{5,1,2,4,3,0:T(8,128)S(1)} %get-tuple-element.80), channel_id=1, source_target_pairs={{0,4},{4,8},{8,12},{12,16},{16,20},{20,24},{24,28},{1,5},{5,9},{9,... | collective-permute-start | bytes 1474568 | tf_op jit(solution)/shard_map/ppermute | solution.py:25
  179.2 3.1 %collective-permute-start.5 = (f32[1,16,3,5,2,256]{5,1,2,0,4,3:T(8,128)S(1)}, f32[1,16,3,5,2,256]{5,1,2,0,4,3:T(8,128)S(1)}, u32[]{:S(2)}, u32[]{:S(2)}) collective-permute-start(f32[1,16,3,5,2,256]{5,1,2,0,4,3:T(8,128)S(1)} %get-tuple-element.81), channel_id=1, source_target_pairs={{4,0},{8,4},{12,8},{16,12},{20,16},{24,20},{28,24},{5,1},{9,5},{13... | collective-permute-start | bytes 1474568 | tf_op jit(solution)/shard_map/ppermute | solution.py:27
  182.4 15.3 %collective-permute-done.4 = f32[1,16,3,5,2,256]{5,1,2,4,3,0:T(8,128)S(1)} collective-permute-done((f32[1,16,3,5,2,256]{5,1,2,4,3,0:T(8,128)S(1)}, f32[1,16,3,5,2,256]{5,1,2,4,3,0:T(8,128)S(1)}, u32[]{:S(2)}, u32[]{:S(2)}) %collective-permute-start.4) | collective-permute-done | bytes 491552 | tf_op jit(solution)/shard_map/ppermute | solution.py:25
  197.7 5.0 %collective-permute-done.5 = f32[1,16,3,5,2,256]{5,1,2,0,4,3:T(8,128)S(1)} collective-permute-done((f32[1,16,3,5,2,256]{5,1,2,0,4,3:T(8,128)S(1)}, f32[1,16,3,5,2,256]{5,1,2,0,4,3:T(8,128)S(1)}, u32[]{:S(2)}, u32[]{:S(2)}) %collective-permute-start.5) | collective-permute-done | bytes 491552 | tf_op jit(solution)/shard_map/ppermute | solution.py:27
  202.6 0.3 pad_maximum_fusion.14
  202.9 3.5 %collective-permute-start.6 = (f32[6,1,3,5,2,256]{5,1,2,0,4,3:T(1,128)S(1)}, f32[6,1,3,5,2,256]{5,1,2,0,4,3:T(1,128)S(1)}, u32[]{:S(2)}, u32[]{:S(2)}) collective-permute-start(f32[6,1,3,5,2,256]{5,1,2,0,4,3:T(1,128)S(1)} %get-tuple-element.74), channel_id=1, source_target_pairs={{0,1},{1,2},{2,3},{4,5},{5,6},{6,7},{8,9},{9,10},{10,11},{12,13},{... | collective-permute-start | bytes 552968 | tf_op jit(solution)/shard_map/ppermute | solution.py:25
  206.4 1.9 collective-permute-start.7
  208.4 0.4 collective-permute-done.6
  208.8 4.4 %collective-permute-done.7 = f32[6,1,3,5,2,256]{5,1,2,0,4,3:T(1,128)S(1)} collective-permute-done((f32[6,1,3,5,2,256]{5,1,2,0,4,3:T(1,128)S(1)}, f32[6,1,3,5,2,256]{5,1,2,0,4,3:T(1,128)S(1)}, u32[]{:S(2)}, u32[]{:S(2)}) %collective-permute-start.7) | collective-permute-done | bytes 184352 | tf_op jit(solution)/shard_map/ppermute | solution.py:27
  213.2 2.9 pad_maximum_fusion.1
  216.1 4.9 %scatter.11 = f32[6,18,3,5,2,256]{5,1,2,0,4,3:T(8,128)} dynamic-update-slice(f32[6,18,3,5,2,256]{5,1,2,0,4,3:T(8,128)} %pad_maximum_fusion.1, f32[1,16,3,5,2,256]{5,1,2,0,4,3:T(8,128)S(1)} %fusion.6, s32[]{:T(128)} %bitcast.17, s32[]{:T(128)} %bitcast.18, s32[]{:T(128)} %constant.117.clone.1, s32[]{:T(128)} %constant.117.clone.1, s32[]{:T(128)} %constant.117.clone.1, s32[]{:T(128)} %constant.117.clone.1) | dynamic-update-slice | bytes 983044 | tf_op jit(solution)/shard_map/scatter | solution.py:132
  221.0 2.2 slice_bitcast_fusion.2
  223.2 6.6 %fusion.116 = (f32[4,16,3,5,2,256]{5,1,2,0,4,3:T(8,128)S(1)}, f32[4,16,3,5,2,256]{5,1,2,0,4,3:T(8,128)S(1)}, f32[4,16,3,5,2,256]{5,1,2,0,4,3:T(8,128)S(1)}) fusion(f32[6,18,3,5,2,256]{5,1,2,0,4,3:T(8,128)} %scatter.11), kind=kLoop, calls=%fused_computation.232 | loop fusion | flops 1966080 | bytes 15728640 | tf_op jit(solution)/shard_map/slice | solution.py:39
  230.1 0.3 fusion.27
  231.0 1.0 copy_subtract_fusion
  232.0 1.9 collective-permute-start.8
  234.0 4.3 %collective-permute-start.9 = (f32[1,16,3,5,2,256]{5,1,4,3,2,0:T(8,128)S(1)}, f32[1,16,3,5,2,256]{5,1,4,3,2,0:T(8,128)S(1)}, u32[]{:S(2)}, u32[]{:S(2)}) collective-permute-start(f32[1,16,3,5,2,256]{5,1,4,3,2,0:T(8,128)S(1)} %get-tuple-element.79), channel_id=1, source_target_pairs={{4,0},{8,4},{12,8},{16,12},{20,16},{24,20},{28,24},{5,1},{9,5},{13... | collective-permute-start | bytes 1474568 | tf_op jit(solution)/shard_map/ppermute | solution.py:27
  238.2 14.1 %collective-permute-done.8 = f32[1,16,3,5,2,256]{5,1,4,3,2,0:T(8,128)S(1)} collective-permute-done((f32[1,16,3,5,2,256]{5,1,4,3,2,0:T(8,128)S(1)}, f32[1,16,3,5,2,256]{5,1,4,3,2,0:T(8,128)S(1)}, u32[]{:S(2)}, u32[]{:S(2)}) %collective-permute-start.8) | collective-permute-done | bytes 491552 | tf_op jit(solution)/shard_map/ppermute | solution.py:25
  252.4 3.1 %collective-permute-done.9 = f32[1,16,3,5,2,256]{5,1,4,3,2,0:T(8,128)S(1)} collective-permute-done((f32[1,16,3,5,2,256]{5,1,4,3,2,0:T(8,128)S(1)}, f32[1,16,3,5,2,256]{5,1,4,3,2,0:T(8,128)S(1)}, u32[]{:S(2)}, u32[]{:S(2)}) %collective-permute-start.9) | collective-permute-done | bytes 491552 | tf_op jit(solution)/shard_map/ppermute | solution.py:27
  255.5 0.3 pad_maximum_fusion.11
  255.7 1.9 collective-permute-start.10
  257.6 2.6 collective-permute-start.11
  260.4 4.1 %collective-permute-done.11 = f32[6,1,3,5,2,256]{5,1,4,3,2,0:T(1,128)S(1)} collective-permute-done((f32[6,1,3,5,2,256]{5,1,4,3,2,0:T(1,128)S(1)}, f32[6,1,3,5,2,256]{5,1,4,3,2,0:T(1,128)S(1)}, u32[]{:S(2)}, u32[]{:S(2)}) %collective-permute-start.11) | collective-permute-done | bytes 184352 | tf_op jit(solution)/shard_map/ppermute | solution.py:27
  264.5 2.8 pad_maximum_fusion.2
  267.3 4.9 %scatter.14 = f32[6,18,3,5,2,256]{5,1,4,3,2,0:T(8,128)} dynamic-update-slice(f32[6,18,3,5,2,256]{5,1,4,3,2,0:T(8,128)} %pad_maximum_fusion.2, f32[1,16,3,5,2,256]{5,1,4,3,2,0:T(8,128)S(1)} %fusion.5, s32[]{:T(128)} %bitcast.17, s32[]{:T(128)} %bitcast.18, s32[]{:T(128)} %constant.117.clone.1, s32[]{:T(128)} %constant.117.clone.1, s32[]{:T(128)} %constant.117.clone.1, s32[]{:T(128)} %constant.117.clone.1) | dynamic-update-slice | bytes 983044 | tf_op jit(solution)/shard_map/scatter | solution.py:132
  272.2 3.1 %slice_bitcast_fusion.1 = (f32[4,16,3,2,256]{4,1,3,2,0:T(8,128)S(1)}, f32[4,16,3,1,2,256]{5,1,4,3,2,0:T(8,128)}, f32[4,16,3,1,2,256]{5,1,4,3,2,0:T(8,128)}, f32[...) fusion(f32[6,18,3,5,2,256]{5,1,4,3,2,0:T(8,128)} %scatter.14), kind=kLoop, calls=%fused_computation.29 | loop fusion | bytes 3932160 | tf_op jit(solution)/shard_map/squeeze | solution.py:53
  275.4 2.9 fusion.115
  278.3 1.0 copy.83
  279.5 1.3 copy-done.3
  280.9 0.6 copy-done.4
  281.5 0.5 subtract_multiply_fusion.1
  281.9 0.5 subtract_multiply_fusion
  282.4 0.5 copy-done.6
  282.9 0.3 fusion.17
  283.9 1.2 copy-done.5
  285.1 1.5 multiply_subtract_fusion
  286.6 2.8 copy.36
  (75 shorter events, 2.9 us)
Async XLA Ops:
  6.5 15.5 %copy-start = (f32[32,32]{1,0:T(8,128)S(1)}, f32[32,32]{1,0:T(8,128)}, u32[]{:S(2)}) copy-start(f32[32,32]{1,0:T(8,128)} %param.19) | copy-start | bytes 12292
  6.5 147.1 %all-reduce.2.cloned.1.call-start = ((), (), s32[]{:S(2)}) async-start(), calls=%async_computation | async-start | bytes 1966080 | tf_op jit(solution)/shard_map/psum | solution.py:120
  7.8 9.7 %copy-start.12 = (s32[256]{0:T(256)S(1)}, s32[256]{0:T(256)}, u32[]{:S(2)}) copy-start(s32[256]{0:T(256)} %param.18) | copy-start | bytes 3076
  7.8 9.8 %copy-start.7 = (f32[128,7,5,32]{0,3,2,1:T(8,128)S(1)}, f32[128,7,5,32]{0,3,2,1:T(8,128)}, u32[]{:S(2)}) copy-start(f32[128,7,5,32]{0,3,2,1:T(8,128)} %param.15) | copy-start | bytes 1720324
  7.8 24.4 %collective-permute-start = (f32[1,16,3,5,2,256]{5,1,2,4,3,0:T(8,128)S(1)}, f32[1,16,3,5,2,256]{5,1,2,4,3,0:T(8,128)S(1)}, u32[]{:S(2)}, u32[]{:S(2)}) collective-permute-start(f32[1,16,3,5,2,256]{5,1,2,4,3,0:T(8,128)S(1)} %copy.42), channel_id=1, source_target_pairs={{0,4},{4,8},{8,12},{12,16},{16,20},{20,24},{24,28},{1,5},{5,9},{9,... | collective-permute-start | bytes 1474568 | tf_op jit(solution)/shard_map/ppermute | solution.py:25
  13.0 5.9 %copy-start.11 = (s32[128]{0:T(128)S(1)}, s32[128]{0:T(128)}, u32[]{:S(2)}) copy-start(s32[128]{0:T(128)} %param.16) | copy-start | bytes 1540
  13.8 21.3 %collective-permute-start.1 = (f32[1,16,3,5,2,256]{5,1,2,0,4,3:T(8,128)}, f32[1,16,3,5,2,256]{5,1,2,0,4,3:T(8,128)S(1)}, u32[]{:S(2)}, u32[]{:S(2)}) collective-permute-start(f32[1,16,3,5,2,256]{5,1,2,0,4,3:T(8,128)} %slice.556), channel_id=1, source_target_pairs={{4,0},{8,4},{12,8},{16,12},{20,16},{24,20},{28,24},{5,1},{9,5},{13... | collective-permute-start | bytes 1474568 | tf_op jit(solution)/shard_map/ppermute | solution.py:27
  24.0 129.7 %copy-start.10 = (f32[64,32]{0,1:T(8,128)S(1)}, f32[64,32]{0,1:T(8,128)}, u32[]{:S(2)}) copy-start(f32[64,32]{0,1:T(8,128)} %param.20) | copy-start | bytes 24580
  36.2 120.2 %collective-permute-start.2 = (f32[6,1,3,5,2,256]{5,1,2,0,4,3:T(1,128)}, f32[6,1,3,5,2,256]{5,1,2,0,4,3:T(1,128)}, u32[]{:S(2)}, u32[]{:S(2)}) collective-permute-start(f32[6,1,3,5,2,256]{5,1,2,0,4,3:T(1,128)} %get-tuple-element.76), channel_id=1, source_target_pairs={{0,1},{1,2},{2,3},{4,5},{5,6},{6,7},{8,9},{9,10},{10,11},{12,13},{... | collective-permute-start | bytes 552968 | tf_op jit(solution)/shard_map/ppermute | solution.py:25
  39.7 116.7 %collective-permute-start.3 = (f32[6,1,3,5,2,256]{5,1,2,0,4,3:T(1,128)}, f32[6,1,3,5,2,256]{5,1,2,0,4,3:T(1,128)}, u32[]{:S(2)}, u32[]{:S(2)}) collective-permute-start(f32[6,1,3,5,2,256]{5,1,2,0,4,3:T(1,128)} %get-tuple-element.77), channel_id=1, source_target_pairs={{1,0},{2,1},{3,2},{5,4},{6,5},{7,6},{9,8},{10,9},{11,10},{13,12},{... | collective-permute-start | bytes 552968 | tf_op jit(solution)/shard_map/ppermute | solution.py:27
  165.2 8.0 %slice-start.2 = ((s8[4423680]{0:T(1024)(128)(4,1)}), s8[4194304]{0:T(1024)(128)(4,1)S(1)}, s32[]{:S(2)}) async-start(s8[4423680]{0:T(1024)(128)(4,1)} %bitcast.163), calls=%async_computation.3 | async-start | bytes 8388608
  167.5 5.7 %slice-start.3 = ((s8[4423680]{0:T(1024)(128)(4,1)}), s8[229376]{0:T(1024)(128)(4,1)S(1)}, s32[]{:S(2)}) async-start(s8[4423680]{0:T(1024)(128)(4,1)} %bitcast.163), calls=%async_computation.4 | async-start | bytes 458752
  173.0 0.7 copy-start.8
  174.2 0.7 copy-start.9
  176.0 21.7 %collective-permute-start.4 = (f32[1,16,3,5,2,256]{5,1,2,4,3,0:T(8,128)S(1)}, f32[1,16,3,5,2,256]{5,1,2,4,3,0:T(8,128)S(1)}, u32[]{:S(2)}, u32[]{:S(2)}) collective-permute-start(f32[1,16,3,5,2,256]{5,1,2,4,3,0:T(8,128)S(1)} %get-tuple-element.80), channel_id=1, source_target_pairs={{0,4},{4,8},{8,12},{12,16},{16,20},{20,24},{24,28},{1,5},{5,9},{9,... | collective-permute-start | bytes 1474568 | tf_op jit(solution)/shard_map/ppermute | solution.py:25
  179.2 23.4 %collective-permute-start.5 = (f32[1,16,3,5,2,256]{5,1,2,0,4,3:T(8,128)S(1)}, f32[1,16,3,5,2,256]{5,1,2,0,4,3:T(8,128)S(1)}, u32[]{:S(2)}, u32[]{:S(2)}) collective-permute-start(f32[1,16,3,5,2,256]{5,1,2,0,4,3:T(8,128)S(1)} %get-tuple-element.81), channel_id=1, source_target_pairs={{4,0},{8,4},{12,8},{16,12},{20,16},{24,20},{28,24},{5,1},{9,5},{13... | collective-permute-start | bytes 1474568 | tf_op jit(solution)/shard_map/ppermute | solution.py:27
  202.9 5.9 %collective-permute-start.6 = (f32[6,1,3,5,2,256]{5,1,2,0,4,3:T(1,128)S(1)}, f32[6,1,3,5,2,256]{5,1,2,0,4,3:T(1,128)S(1)}, u32[]{:S(2)}, u32[]{:S(2)}) collective-permute-start(f32[6,1,3,5,2,256]{5,1,2,0,4,3:T(1,128)S(1)} %get-tuple-element.74), channel_id=1, source_target_pairs={{0,1},{1,2},{2,3},{4,5},{5,6},{6,7},{8,9},{9,10},{10,11},{12,13},{... | collective-permute-start | bytes 552968 | tf_op jit(solution)/shard_map/ppermute | solution.py:25
  206.4 6.9 %collective-permute-start.7 = (f32[6,1,3,5,2,256]{5,1,2,0,4,3:T(1,128)S(1)}, f32[6,1,3,5,2,256]{5,1,2,0,4,3:T(1,128)S(1)}, u32[]{:S(2)}, u32[]{:S(2)}) collective-permute-start(f32[6,1,3,5,2,256]{5,1,2,0,4,3:T(1,128)S(1)} %get-tuple-element.75), channel_id=1, source_target_pairs={{1,0},{2,1},{3,2},{5,4},{6,5},{7,6},{9,8},{10,9},{11,10},{13,12},{... | collective-permute-start | bytes 552968 | tf_op jit(solution)/shard_map/ppermute | solution.py:27
  221.0 9.0 %slice-start = ((s8[4423680]{0:T(1024)(128)(4,1)}), s8[4194304]{0:T(1024)(128)(4,1)S(1)}, s32[]{:S(2)}) async-start(s8[4423680]{0:T(1024)(128)(4,1)} %bitcast.161), calls=%async_computation.1 | async-start | bytes 8388608
  223.2 6.8 %slice-start.1 = ((s8[4423680]{0:T(1024)(128)(4,1)}), s8[229376]{0:T(1024)(128)(4,1)S(1)}, s32[]{:S(2)}) async-start(s8[4423680]{0:T(1024)(128)(4,1)} %bitcast.161), calls=%async_computation.2 | async-start | bytes 458752
  232.0 20.3 %collective-permute-start.8 = (f32[1,16,3,5,2,256]{5,1,4,3,2,0:T(8,128)S(1)}, f32[1,16,3,5,2,256]{5,1,4,3,2,0:T(8,128)S(1)}, u32[]{:S(2)}, u32[]{:S(2)}) collective-permute-start(f32[1,16,3,5,2,256]{5,1,4,3,2,0:T(8,128)S(1)} %get-tuple-element.78), channel_id=1, source_target_pairs={{0,4},{4,8},{8,12},{12,16},{16,20},{20,24},{24,28},{1,5},{5,9},{9,... | collective-permute-start | bytes 1474568 | tf_op jit(solution)/shard_map/ppermute | solution.py:25
  234.0 21.5 %collective-permute-start.9 = (f32[1,16,3,5,2,256]{5,1,4,3,2,0:T(8,128)S(1)}, f32[1,16,3,5,2,256]{5,1,4,3,2,0:T(8,128)S(1)}, u32[]{:S(2)}, u32[]{:S(2)}) collective-permute-start(f32[1,16,3,5,2,256]{5,1,4,3,2,0:T(8,128)S(1)} %get-tuple-element.79), channel_id=1, source_target_pairs={{4,0},{8,4},{12,8},{16,12},{20,16},{24,20},{28,24},{5,1},{9,5},{13... | collective-permute-start | bytes 1474568 | tf_op jit(solution)/shard_map/ppermute | solution.py:27
  255.7 4.7 %collective-permute-start.10 = (f32[6,1,3,5,2,256]{5,1,4,3,2,0:T(1,128)S(1)}, f32[6,1,3,5,2,256]{5,1,4,3,2,0:T(1,128)S(1)}, u32[]{:S(2)}, u32[]{:S(2)}) collective-permute-start(f32[6,1,3,5,2,256]{5,1,4,3,2,0:T(1,128)S(1)} %get-tuple-element.72), channel_id=1, source_target_pairs={{0,1},{1,2},{2,3},{4,5},{5,6},{6,7},{8,9},{9,10},{10,11},{12,13},{... | collective-permute-start | bytes 552968 | tf_op jit(solution)/shard_map/ppermute | solution.py:25
  257.6 6.9 %collective-permute-start.11 = (f32[6,1,3,5,2,256]{5,1,4,3,2,0:T(1,128)S(1)}, f32[6,1,3,5,2,256]{5,1,4,3,2,0:T(1,128)S(1)}, u32[]{:S(2)}, u32[]{:S(2)}) collective-permute-start(f32[6,1,3,5,2,256]{5,1,4,3,2,0:T(1,128)S(1)} %get-tuple-element.73), channel_id=1, source_target_pairs={{1,0},{2,1},{3,2},{5,4},{6,5},{7,6},{9,8},{10,9},{11,10},{13,12},{... | collective-permute-start | bytes 552968 | tf_op jit(solution)/shard_map/ppermute | solution.py:27
  272.2 3.2 %copy-start.2 = (f32[6,18,3,5,2,256]{5,1,4,3,2,0:T(8,128)S(1)}, f32[6,18,3,5,2,256]{5,1,4,3,2,0:T(8,128)}, u32[]{:S(2)}) copy-start(f32[6,18,3,5,2,256]{5,1,4,3,2,0:T(8,128)} %scatter.14) | copy-start | bytes 9953284
  279.3 1.5 copy-start.3
  279.3 2.1 copy-start.4
  281.9 1.0 copy-start.6
  283.6 1.5 copy-start.5
  285.1 4.3 %copy-start.1 = (f32[32,32]{1,0:T(8,128)S(1)}, f32[32,32]{1,0:T(8,128)}, u32[]{:S(2)}) copy-start(f32[32,32]{1,0:T(8,128)} %param.19) | copy-start | bytes 12292
Sparse Core Ops, SparseCore 0:
  24.1 129.4 all-reduce.1
where the time goes:
time: 297 us; the launch traced here: 296 us
  waiting for transfers between devices  169 us (57%)
  local copies, waits for them, and re-layouts  38.5 us (13%)
  starting transfers between devices  34.2 us (12%)
  other arithmetic  32.1 us (11%)
  between operations  14.7 us (5%)
  matrix products  7.93 us (3%)
    psum x1, waiting for transfers between devices, on_device(): totals = lax.psum(partial_value, ('ax', 'rad'))  112 us
    ppermute x6, waiting for transfers between devices, extended(): lax.ppermute(tail, axis, [(i, (i + 1) % count) for i in range(ends)])  37.4 us
    ppermute x6, waiting for transfers between devices, extended(): lax.ppermute(head, axis, [((i + 1) % count, i) for i in range(ends)])  19.5 us
    ppermute x6, starting transfers between devices, extended(): lax.ppermute(tail, axis, [(i, (i + 1) % count) for i in range(ends)])  17.3 us
    ppermute x6, starting transfers between devices, extended(): lax.ppermute(head, axis, [((i + 1) % count, i) for i in range(ends)])  16.9 us
    scatter x3, local copies, waits for them, and re-layouts, on_device(): padded = padded.at[0, 1:-1].set(ghost)  14.8 us
    concatenate x3, other arithmetic, extended(): jnp.concatenate([lax.ppermute(tail, axis, [(i, (i + 1) % count) for i in...  9.55 us
    unnamed x40, local copies, waits for them, and re-layouts  7.62 us
  transfers between devices with their start and end apart: 13, of which 10 were waited for; matrix products, arithmetic and copies ran while one was open for 5% of the time, Pallas kernels for 0%

commit v1 on v0

--- a/solution.py
+++ b/solution.py
@@ -117,7 +117,7 @@
     partial_value = project(face_data, face_station, valid, wave_orders, radial_proj)
     rows_here = duct_field.shape[1]
     radial_index = lax.axis_index("rad")
-    totals = lax.psum(partial_value, ("ax", "rad"))
+    totals = lax.psum(lax.psum(partial_value, "rad"), "ax")
     shape_rows = lax.dynamic_slice_in_dim(radial_modes, radial_index * rows_here, rows_here, 0)
     boundary = jnp.einsum("jn,nkvcs->jkvcs", shape_rows, totals, precision=lax.Precision.HIGHEST)
     modes = wave_orders.astype(jnp.float32)

time: 297 us -> 271 us (0.912)
  waiting for transfers between devices: 169 us -> 145 us
    psum x1 -> x2, waiting for transfers between devices: 112 us -> 93.7 us  [on_device(): totals = lax.psum(lax.psum(partial_value, 'rad'), 'ax')]
    ppermute x6, waiting for transfers between devices: 37.4 us -> 31.7 us  [extended(): lax.ppermute(tail, axis, [(i, (i + 1) % count) for i in range(ends)])]
    unnamed x40 -> x36, local copies, waits for them, and re-layouts: 7.62 us -> 8.42 us
  transfers between devices with their start and end apart: 13 -> 14, of which waited for: 10 -> 10; matrix products, arithmetic and copies ran while one was open for 5% -> 2% of each run, Pallas kernels for 0% -> 0%
where the time goes in v1:
time: 271 us; the launch traced here: 270 us
  waiting for transfers between devices  145 us (54%)
  local copies, waits for them, and re-layouts  37 us (14%)
  starting transfers between devices  33.9 us (13%)
  other arithmetic  30.2 us (11%)
  between operations  14.7 us (5%)
  matrix products  9.64 us (4%)
    psum x2, waiting for transfers between devices, on_device(): totals = lax.psum(lax.psum(partial_value, 'rad'), 'ax')  93.7 us
    ppermute x6, waiting for transfers between devices, extended(): lax.ppermute(tail, axis, [(i, (i + 1) % count) for i in range(ends)])  31.7 us
    ppermute x6, waiting for transfers between devices, extended(): lax.ppermute(head, axis, [((i + 1) % count, i) for i in range(ends)])  19.3 us
    ppermute x6, starting transfers between devices, extended(): lax.ppermute(tail, axis, [(i, (i + 1) % count) for i in range(ends)])  17.7 us
    ppermute x6, starting transfers between devices, extended(): lax.ppermute(head, axis, [((i + 1) % count, i) for i in range(ends)])  16.1 us
    scatter x3, local copies, waits for them, and re-layouts, on_device(): padded = padded.at[0, 1:-1].set(ghost)  14.7 us
    concatenate x3, other arithmetic, extended(): jnp.concatenate([lax.ppermute(tail, axis, [(i, (i + 1) % count) for i in...  8.6 us
    unnamed x36, local copies, waits for them, and re-layouts  8.42 us
  transfers between devices with their start and end apart: 14, of which 10 were waited for; matrix products, arithmetic and copies ran while one was open for 2% of the time, Pallas kernels for 0%

profile of v1, /device:TPU:9, one launch (start us, length us, event | category | flops | bytes accessed | tf_op | source)
XLA Modules:
  0.0 270.3 jit_solution(2436010545151979610)
XLA Ops:
  7.2 0.7 fusion.111
  8.0 2.3 convolution_bitcast_fusion.1
  10.3 2.1 fusion.47
  12.5 1.5 fusion.49
  14.0 0.2 slice_add_fusion
  14.2 1.9 convolution_bitcast_fusion
  16.1 0.9 copy.42
  17.0 3.1 %collective-permute-start = (f32[1,16,3,5,2,256]{5,1,2,4,3,0:T(8,128)}, f32[1,16,3,5,2,256]{5,1,2,4,3,0:T(8,128)S(1)}, u32[]{:S(2)}, u32[]{:S(2)}) collective-permute-start(f32[1,16,3,5,2,256]{5,1,2,4,3,0:T(8,128)} %copy.42), channel_id=1, source_target_pairs={{0,4},{4,8},{8,12},{12,16},{16,20},{20,24},{24,28},{1,5},{5,9},{9,... | collective-permute-start | bytes 1474568 | tf_op jit(solution)/shard_map/ppermute | solution.py:25
  20.1 1.8 copy.13
  22.0 3.0 %collective-permute-start.1 = (f32[1,16,3,5,2,256]{5,1,2,0,4,3:T(8,128)S(1)}, f32[1,16,3,5,2,256]{5,1,2,0,4,3:T(8,128)S(1)}, u32[]{:S(2)}, u32[]{:S(2)}) collective-permute-start(f32[1,16,3,5,2,256]{5,1,2,0,4,3:T(8,128)S(1)} %slice.556), channel_id=1, source_target_pairs={{4,0},{8,4},{12,8},{16,12},{20,16},{24,20},{28,24},{5,1},{9,5},{13... | collective-permute-start | bytes 1474568 | tf_op jit(solution)/shard_map/ppermute | solution.py:27
  25.1 27.6 %all-reduce.3.cloned.1.call-done = f32[32,3,5,2,256]{4,0,3,2,1:T(8,128)} async-done(((f32[32,3,5,2,256]{4,0,3,2,1:T(8,128)}), f32[32,3,5,2,256]{4,0,3,2,1:T(8,128)}) %all-reduce.3.cloned.1.call-update) | async-done | bytes 983056 | tf_op jit(solution)/shard_map/psum | solution.py:120
  52.7 0.3 pad_maximum_fusion.17
  53.0 3.7 %collective-permute-start.2 = (f32[6,1,3,5,2,256]{5,1,2,0,4,3:T(1,128)S(1)}, f32[6,1,3,5,2,256]{5,1,2,0,4,3:T(1,128)S(1)}, u32[]{:S(2)}, u32[]{:S(2)}) collective-permute-start(f32[6,1,3,5,2,256]{5,1,2,0,4,3:T(1,128)S(1)} %get-tuple-element.76), channel_id=1, source_target_pairs={{0,1},{1,2},{2,3},{4,5},{5,6},{6,7},{8,9},{9,10},{10,11},{12,13},{... | collective-permute-start | bytes 552968 | tf_op jit(solution)/shard_map/ppermute | solution.py:25
  56.7 1.9 collective-permute-start.3
  58.6 0.6 fusion.118
  59.2 4.3 %collective-permute-done.3 = f32[6,1,3,5,2,256]{5,1,2,0,4,3:T(1,128)S(1)} collective-permute-done((f32[6,1,3,5,2,256]{5,1,2,0,4,3:T(1,128)S(1)}, f32[6,1,3,5,2,256]{5,1,2,0,4,3:T(1,128)S(1)}, u32[]{:S(2)}, u32[]{:S(2)}) %collective-permute-start.3) | collective-permute-done | bytes 184352 | tf_op jit(solution)/shard_map/ppermute | solution.py:27
  63.5 2.8 %pad_maximum_fusion = f32[6,18,3,5,2,256]{5,1,2,0,4,3:T(8,128)} fusion(f32[6,1,3,5,2,256]{5,1,2,0,4,3:T(1,128)S(1)} %collective-permute-done.3, f32[1,16,3,5,2,256]{5,1,2,0,4,3:T(8,128)S(1)} %collective-permute-done.1, f32[4,16,3,5,2,256]{5,1,2,0,4,3:T(8,128)S(1)} %copy.13, f32[1,16,3,5,2,256]{5,1,2,0,4,3:T(8,128)S(1)} %bitcast.166, ...), kind=kLoop, calls=%fused_computation | loop fusion | flops 3317760 | bytes 6635520 | tf_op jit(solution)/shard_map/concatenate | solution.py:23
  66.4 66.1 %all-reduce.5.cloned.1.call-done = f32[32,3,5,2,256]{4,0,3,2,1:T(8,128)} async-done(((f32[32,3,5,2,256]{4,0,3,2,1:T(8,128)}), f32[32,3,5,2,256]{4,0,3,2,1:T(8,128)}) %all-reduce.5.cloned.1.call-update) | async-done | bytes 983056 | tf_op jit(solution)/shard_map/psum | solution.py:120
  132.5 1.9 fusion.82
  134.4 4.9 %scatter.10 = f32[6,18,3,5,2,256]{5,1,2,0,4,3:T(8,128)} dynamic-update-slice(f32[6,18,3,5,2,256]{5,1,2,0,4,3:T(8,128)} %pad_maximum_fusion, f32[1,16,3,5,2,256]{5,1,2,0,4,3:T(8,128)S(1)} %fusion.7, s32[]{:T(128)} %bitcast.17, s32[]{:T(128)} %bitcast.18, s32[]{:T(128)} %constant.117.clone.1, s32[]{:T(128)} %constant.117.clone.1, s32[]{:T(128)} %constant.117.clone.1, s32[]{:T(128)} %constant.117.clone.1) | dynamic-update-slice | bytes 983044 | tf_op jit(solution)/shard_map/scatter | solution.py:132
  139.3 2.3 slice_bitcast_fusion.6
  141.6 5.5 %subtract_multiply_fusion.5 = (f32[4,16,3,5,2,256]{5,1,2,0,4,3:T(8,128)S(1)}, f32[4,16,3,5,2,256]{5,1,2,0,4,3:T(8,128)S(1)}) fusion(f32[6,18,3,5,2,256]{5,1,2,0,4,3:T(8,128)} %scatter.10), kind=kLoop, calls=%fused_computation.11 | loop fusion | flops 1966080 | bytes 11796480 | tf_op jit(solution)/shard_map/mul | solution.py:41
  147.3 0.4 copy-done.7
  147.8 0.3 fusion.37
  148.7 0.4 copy-done.8
  149.1 1.0 multiply_subtract_fusion.1
  150.1 3.2 %collective-permute-start.4 = (f32[1,16,3,5,2,256]{5,1,2,4,3,0:T(8,128)S(1)}, f32[1,16,3,5,2,256]{5,1,2,4,3,0:T(8,128)S(1)}, u32[]{:S(2)}, u32[]{:S(2)}) collective-permute-start(f32[1,16,3,5,2,256]{5,1,2,4,3,0:T(8,128)S(1)} %get-tuple-element.80), channel_id=1, source_target_pairs={{0,4},{4,8},{8,12},{12,16},{16,20},{20,24},{24,28},{1,5},{5,9},{9,... | collective-permute-start | bytes 1474568 | tf_op jit(solution)/shard_map/ppermute | solution.py:25
  153.3 3.0 %collective-permute-start.5 = (f32[1,16,3,5,2,256]{5,1,2,0,4,3:T(8,128)S(1)}, f32[1,16,3,5,2,256]{5,1,2,0,4,3:T(8,128)S(1)}, u32[]{:S(2)}, u32[]{:S(2)}) collective-permute-start(f32[1,16,3,5,2,256]{5,1,2,0,4,3:T(8,128)S(1)} %get-tuple-element.81), channel_id=1, source_target_pairs={{4,0},{8,4},{12,8},{16,12},{20,16},{24,20},{28,24},{5,1},{9,5},{13... | collective-permute-start | bytes 1474568 | tf_op jit(solution)/shard_map/ppermute | solution.py:27
  156.3 16.7 %collective-permute-done.4 = f32[1,16,3,5,2,256]{5,1,2,4,3,0:T(8,128)S(1)} collective-permute-done((f32[1,16,3,5,2,256]{5,1,2,4,3,0:T(8,128)S(1)}, f32[1,16,3,5,2,256]{5,1,2,4,3,0:T(8,128)S(1)}, u32[]{:S(2)}, u32[]{:S(2)}) %collective-permute-start.4) | collective-permute-done | bytes 491552 | tf_op jit(solution)/shard_map/ppermute | solution.py:25
  173.0 3.6 %collective-permute-done.5 = f32[1,16,3,5,2,256]{5,1,2,0,4,3:T(8,128)S(1)} collective-permute-done((f32[1,16,3,5,2,256]{5,1,2,0,4,3:T(8,128)S(1)}, f32[1,16,3,5,2,256]{5,1,2,0,4,3:T(8,128)S(1)}, u32[]{:S(2)}, u32[]{:S(2)}) %collective-permute-start.5) | collective-permute-done | bytes 491552 | tf_op jit(solution)/shard_map/ppermute | solution.py:27
  176.6 0.3 pad_maximum_fusion.14
  176.8 3.5 %collective-permute-start.6 = (f32[6,1,3,5,2,256]{5,1,2,0,4,3:T(1,128)S(1)}, f32[6,1,3,5,2,256]{5,1,2,0,4,3:T(1,128)S(1)}, u32[]{:S(2)}, u32[]{:S(2)}) collective-permute-start(f32[6,1,3,5,2,256]{5,1,2,0,4,3:T(1,128)S(1)} %get-tuple-element.74), channel_id=1, source_target_pairs={{0,1},{1,2},{2,3},{4,5},{5,6},{6,7},{8,9},{9,10},{10,11},{12,13},{... | collective-permute-start | bytes 552968 | tf_op jit(solution)/shard_map/ppermute | solution.py:25
  180.3 1.9 collective-permute-start.7
  182.3 0.5 collective-permute-done.6
  182.8 4.4 %collective-permute-done.7 = f32[6,1,3,5,2,256]{5,1,2,0,4,3:T(1,128)S(1)} collective-permute-done((f32[6,1,3,5,2,256]{5,1,2,0,4,3:T(1,128)S(1)}, f32[6,1,3,5,2,256]{5,1,2,0,4,3:T(1,128)S(1)}, u32[]{:S(2)}, u32[]{:S(2)}) %collective-permute-start.7) | collective-permute-done | bytes 184352 | tf_op jit(solution)/shard_map/ppermute | solution.py:27
  187.2 2.8 %pad_maximum_fusion.1 = f32[6,18,3,5,2,256]{5,1,2,0,4,3:T(8,128)} fusion(f32[6,1,3,5,2,256]{5,1,2,0,4,3:T(1,128)S(1)} %collective-permute-done.7, f32[1,16,3,5,2,256]{5,1,2,0,4,3:T(8,128)S(1)} %collective-permute-done.5, f32[4,16,3,5,2,256]{5,1,2,0,4,3:T(8,128)S(1)} %multiply_subtract_fusion.1, f32[1,16,3,5,2,256]{5,1,2,0,4,3:T(8,128)S(1)} %bitcast.168, ...), kind=kLoop, calls=%fused_computation.1 | loop fusion | flops 3317760 | bytes 6635520 | tf_op jit(solution)/shard_map/concatenate | solution.py:23
  190.0 4.9 %scatter.11 = f32[6,18,3,5,2,256]{5,1,2,0,4,3:T(8,128)} dynamic-update-slice(f32[6,18,3,5,2,256]{5,1,2,0,4,3:T(8,128)} %pad_maximum_fusion.1, f32[1,16,3,5,2,256]{5,1,2,0,4,3:T(8,128)S(1)} %fusion.6, s32[]{:T(128)} %bitcast.17, s32[]{:T(128)} %bitcast.18, s32[]{:T(128)} %constant.117.clone.1, s32[]{:T(128)} %constant.117.clone.1, s32[]{:T(128)} %constant.117.clone.1, s32[]{:T(128)} %constant.117.clone.1) | dynamic-update-slice | bytes 983044 | tf_op jit(solution)/shard_map/scatter | solution.py:132
  194.9 2.2 slice_bitcast_fusion.2
  197.1 6.6 %fusion.116 = (f32[4,16,3,5,2,256]{5,1,2,0,4,3:T(8,128)S(1)}, f32[4,16,3,5,2,256]{5,1,2,0,4,3:T(8,128)S(1)}, f32[4,16,3,5,2,256]{5,1,2,0,4,3:T(8,128)S(1)}) fusion(f32[6,18,3,5,2,256]{5,1,2,0,4,3:T(8,128)} %scatter.11), kind=kLoop, calls=%fused_computation.232 | loop fusion | flops 1966080 | bytes 15728640 | tf_op jit(solution)/shard_map/slice | solution.py:39
  204.0 0.3 fusion.27
  204.6 0.2 fusion.20
  204.9 1.0 copy_subtract_fusion
  205.9 2.3 collective-permute-start.8
  208.3 3.9 %collective-permute-start.9 = (f32[1,16,3,5,2,256]{5,1,4,3,2,0:T(8,128)S(1)}, f32[1,16,3,5,2,256]{5,1,4,3,2,0:T(8,128)S(1)}, u32[]{:S(2)}, u32[]{:S(2)}) collective-permute-start(f32[1,16,3,5,2,256]{5,1,4,3,2,0:T(8,128)S(1)} %get-tuple-element.79), channel_id=1, source_target_pairs={{4,0},{8,4},{12,8},{16,12},{20,16},{24,20},{28,24},{5,1},{9,5},{13... | collective-permute-start | bytes 1474568 | tf_op jit(solution)/shard_map/ppermute | solution.py:27
  212.1 14.6 %collective-permute-done.8 = f32[1,16,3,5,2,256]{5,1,4,3,2,0:T(8,128)S(1)} collective-permute-done((f32[1,16,3,5,2,256]{5,1,4,3,2,0:T(8,128)S(1)}, f32[1,16,3,5,2,256]{5,1,4,3,2,0:T(8,128)S(1)}, u32[]{:S(2)}, u32[]{:S(2)}) %collective-permute-start.8) | collective-permute-done | bytes 491552 | tf_op jit(solution)/shard_map/ppermute | solution.py:25
  226.8 2.6 collective-permute-done.9
  229.4 0.3 pad_maximum_fusion.11
  229.6 1.9 collective-permute-start.10
  231.5 2.4 collective-permute-start.11
  234.1 4.3 %collective-permute-done.11 = f32[6,1,3,5,2,256]{5,1,4,3,2,0:T(1,128)S(1)} collective-permute-done((f32[6,1,3,5,2,256]{5,1,4,3,2,0:T(1,128)S(1)}, f32[6,1,3,5,2,256]{5,1,4,3,2,0:T(1,128)S(1)}, u32[]{:S(2)}, u32[]{:S(2)}) %collective-permute-start.11) | collective-permute-done | bytes 184352 | tf_op jit(solution)/shard_map/ppermute | solution.py:27
  238.4 2.9 %pad_maximum_fusion.2 = f32[6,18,3,5,2,256]{5,1,4,3,2,0:T(8,128)} fusion(f32[6,1,3,5,2,256]{5,1,4,3,2,0:T(1,128)S(1)} %collective-permute-done.11, f32[1,16,3,5,2,256]{5,1,4,3,2,0:T(8,128)S(1)} %collective-permute-done.9, f32[4,16,3,5,2,256]{5,1,4,3,2,0:T(8,128)S(1)} %copy_subtract_fusion, f32[1,16,3,5,2,256]{5,1,4,3,2,0:T(8,128)S(1)} %collective-permute-done.8, ...), kind=kLoop, calls=%fused_computation.2 | loop fusion | flops 3317760 | bytes 6635520 | tf_op jit(solution)/shard_map/concatenate | solution.py:23
  241.3 4.9 %scatter.14 = f32[6,18,3,5,2,256]{5,1,4,3,2,0:T(8,128)} dynamic-update-slice(f32[6,18,3,5,2,256]{5,1,4,3,2,0:T(8,128)} %pad_maximum_fusion.2, f32[1,16,3,5,2,256]{5,1,4,3,2,0:T(8,128)S(1)} %fusion.5, s32[]{:T(128)} %bitcast.17, s32[]{:T(128)} %bitcast.18, s32[]{:T(128)} %constant.117.clone.1, s32[]{:T(128)} %constant.117.clone.1, s32[]{:T(128)} %constant.117.clone.1, s32[]{:T(128)} %constant.117.clone.1) | dynamic-update-slice | bytes 983044 | tf_op jit(solution)/shard_map/scatter | solution.py:132
  246.2 3.1 %slice_bitcast_fusion.1 = (f32[4,16,3,2,256]{4,1,3,2,0:T(8,128)S(1)}, f32[4,16,3,1,2,256]{5,1,4,3,2,0:T(8,128)}, f32[4,16,3,1,2,256]{5,1,4,3,2,0:T(8,128)}, f32[...) fusion(f32[6,18,3,5,2,256]{5,1,4,3,2,0:T(8,128)} %scatter.14), kind=kLoop, calls=%fused_computation.29 | loop fusion | bytes 3932160 | tf_op jit(solution)/shard_map/squeeze | solution.py:53
  249.4 2.9 %fusion.115 = (f32[4,16,3,5,2,256]{5,1,4,3,2,0:T(8,128)}, f32[4,16,3,5,2,256]{5,1,4,3,2,0:T(8,128)S(1)}, f32[4,16,3,5,2,256]{5,1,4,3,2,0:T(8,128)S(1)}, f32[4,16...) fusion(f32[6,18,3,5,2,256]{5,1,4,3,2,0:T(8,128)S(1)} %copy-done.2), kind=kLoop, calls=%fused_computation.231 | loop fusion | bytes 19660800 | tf_op jit(solution)/shard_map/slice | solution.py:39
  252.3 1.0 copy.83
  253.5 1.3 copy-done.3
  254.9 0.6 copy-done.4
  255.4 0.5 subtract_multiply_fusion.1
  255.9 0.5 subtract_multiply_fusion
  256.4 0.5 copy-done.6
  256.9 0.3 fusion.17
  257.9 1.2 copy-done.5
  259.1 1.5 multiply_subtract_fusion
  260.6 2.8 %copy.36 = f32[4,16,3,5,2,256]{5,4,3,2,1,0:T(2,128)} copy(f32[4,16,3,5,2,256]{5,1,2,0,4,3:T(8,128)S(1)} %multiply_subtract_fusion) | data formatting | bytes 3932160 | tf_op jit(solution)/shard_map/sub | solution.py:71
  (75 shorter events, 2.9 us)
Async XLA Ops:
  6.5 7.6 %copy-start = (f32[32,32]{1,0:T(8,128)S(1)}, f32[32,32]{1,0:T(8,128)}, u32[]{:S(2)}) copy-start(f32[32,32]{1,0:T(8,128)} %param.19) | copy-start | bytes 12292
  6.5 5.9 %copy-start.10 = (s32[128]{0:T(128)S(1)}, s32[128]{0:T(128)}, u32[]{:S(2)}) copy-start(s32[128]{0:T(128)} %param.16) | copy-start | bytes 1540
  6.5 46.1 %all-reduce.3.cloned.1.call-start = ((), (), s32[]{:S(2)}) async-start(), calls=%async_computation | async-start | bytes 1966080 | tf_op jit(solution)/shard_map/psum | solution.py:120
  14.1 2.0 slice-start.4
  16.1 116.4 %all-reduce.5.cloned.1.call-start = ((), (), s32[]{:S(2)}) async-start(), calls=%async_computation.1 | async-start | bytes 1966080 | tf_op jit(solution)/shard_map/psum | solution.py:120
  17.0 35.7 %collective-permute-start = (f32[1,16,3,5,2,256]{5,1,2,4,3,0:T(8,128)}, f32[1,16,3,5,2,256]{5,1,2,4,3,0:T(8,128)S(1)}, u32[]{:S(2)}, u32[]{:S(2)}) collective-permute-start(f32[1,16,3,5,2,256]{5,1,2,4,3,0:T(8,128)} %copy.42), channel_id=1, source_target_pairs={{0,4},{4,8},{8,12},{12,16},{16,20},{20,24},{24,28},{1,5},{5,9},{9,... | collective-permute-start | bytes 1474568 | tf_op jit(solution)/shard_map/ppermute | solution.py:25
  22.0 30.7 %collective-permute-start.1 = (f32[1,16,3,5,2,256]{5,1,2,0,4,3:T(8,128)S(1)}, f32[1,16,3,5,2,256]{5,1,2,0,4,3:T(8,128)S(1)}, u32[]{:S(2)}, u32[]{:S(2)}) collective-permute-start(f32[1,16,3,5,2,256]{5,1,2,0,4,3:T(8,128)S(1)} %slice.556), channel_id=1, source_target_pairs={{4,0},{8,4},{12,8},{16,12},{20,16},{24,20},{28,24},{5,1},{9,5},{13... | collective-permute-start | bytes 1474568 | tf_op jit(solution)/shard_map/ppermute | solution.py:27
  53.0 6.2 %collective-permute-start.2 = (f32[6,1,3,5,2,256]{5,1,2,0,4,3:T(1,128)S(1)}, f32[6,1,3,5,2,256]{5,1,2,0,4,3:T(1,128)S(1)}, u32[]{:S(2)}, u32[]{:S(2)}) collective-permute-start(f32[6,1,3,5,2,256]{5,1,2,0,4,3:T(1,128)S(1)} %get-tuple-element.76), channel_id=1, source_target_pairs={{0,1},{1,2},{2,3},{4,5},{5,6},{6,7},{8,9},{9,10},{10,11},{12,13},{... | collective-permute-start | bytes 552968 | tf_op jit(solution)/shard_map/ppermute | solution.py:25
  56.7 6.9 %collective-permute-start.3 = (f32[6,1,3,5,2,256]{5,1,2,0,4,3:T(1,128)S(1)}, f32[6,1,3,5,2,256]{5,1,2,0,4,3:T(1,128)S(1)}, u32[]{:S(2)}, u32[]{:S(2)}) collective-permute-start(f32[6,1,3,5,2,256]{5,1,2,0,4,3:T(1,128)S(1)} %get-tuple-element.77), channel_id=1, source_target_pairs={{1,0},{2,1},{3,2},{5,4},{6,5},{7,6},{9,8},{10,9},{11,10},{13,12},{... | collective-permute-start | bytes 552968 | tf_op jit(solution)/shard_map/ppermute | solution.py:27
  59.2 73.3 %copy-start.9 = (f32[64,32]{0,1:T(8,128)S(1)}, f32[64,32]{0,1:T(8,128)}, u32[]{:S(2)}) copy-start(f32[64,32]{0,1:T(8,128)} %param.20) | copy-start | bytes 24580
  139.3 8.0 %slice-start.2 = ((s8[4423680]{0:T(1024)(128)(4,1)}), s8[4194304]{0:T(1024)(128)(4,1)S(1)}, s32[]{:S(2)}) async-start(s8[4423680]{0:T(1024)(128)(4,1)} %bitcast.163), calls=%async_computation.4 | async-start | bytes 8388608
  141.6 5.7 %slice-start.3 = ((s8[4423680]{0:T(1024)(128)(4,1)}), s8[229376]{0:T(1024)(128)(4,1)S(1)}, s32[]{:S(2)}) async-start(s8[4423680]{0:T(1024)(128)(4,1)} %bitcast.163), calls=%async_computation.5 | async-start | bytes 458752
  147.1 0.7 copy-start.7
  148.4 0.7 copy-start.8
  150.1 22.9 %collective-permute-start.4 = (f32[1,16,3,5,2,256]{5,1,2,4,3,0:T(8,128)S(1)}, f32[1,16,3,5,2,256]{5,1,2,4,3,0:T(8,128)S(1)}, u32[]{:S(2)}, u32[]{:S(2)}) collective-permute-start(f32[1,16,3,5,2,256]{5,1,2,4,3,0:T(8,128)S(1)} %get-tuple-element.80), channel_id=1, source_target_pairs={{0,4},{4,8},{8,12},{12,16},{16,20},{20,24},{24,28},{1,5},{5,9},{9,... | collective-permute-start | bytes 1474568 | tf_op jit(solution)/shard_map/ppermute | solution.py:25
  153.3 23.3 %collective-permute-start.5 = (f32[1,16,3,5,2,256]{5,1,2,0,4,3:T(8,128)S(1)}, f32[1,16,3,5,2,256]{5,1,2,0,4,3:T(8,128)S(1)}, u32[]{:S(2)}, u32[]{:S(2)}) collective-permute-start(f32[1,16,3,5,2,256]{5,1,2,0,4,3:T(8,128)S(1)} %get-tuple-element.81), channel_id=1, source_target_pairs={{4,0},{8,4},{12,8},{16,12},{20,16},{24,20},{28,24},{5,1},{9,5},{13... | collective-permute-start | bytes 1474568 | tf_op jit(solution)/shard_map/ppermute | solution.py:27
  176.8 5.9 %collective-permute-start.6 = (f32[6,1,3,5,2,256]{5,1,2,0,4,3:T(1,128)S(1)}, f32[6,1,3,5,2,256]{5,1,2,0,4,3:T(1,128)S(1)}, u32[]{:S(2)}, u32[]{:S(2)}) collective-permute-start(f32[6,1,3,5,2,256]{5,1,2,0,4,3:T(1,128)S(1)} %get-tuple-element.74), channel_id=1, source_target_pairs={{0,1},{1,2},{2,3},{4,5},{5,6},{6,7},{8,9},{9,10},{10,11},{12,13},{... | collective-permute-start | bytes 552968 | tf_op jit(solution)/shard_map/ppermute | solution.py:25
  180.3 6.9 %collective-permute-start.7 = (f32[6,1,3,5,2,256]{5,1,2,0,4,3:T(1,128)S(1)}, f32[6,1,3,5,2,256]{5,1,2,0,4,3:T(1,128)S(1)}, u32[]{:S(2)}, u32[]{:S(2)}) collective-permute-start(f32[6,1,3,5,2,256]{5,1,2,0,4,3:T(1,128)S(1)} %get-tuple-element.75), channel_id=1, source_target_pairs={{1,0},{2,1},{3,2},{5,4},{6,5},{7,6},{9,8},{10,9},{11,10},{13,12},{... | collective-permute-start | bytes 552968 | tf_op jit(solution)/shard_map/ppermute | solution.py:27
  194.9 9.0 %slice-start = ((s8[4423680]{0:T(1024)(128)(4,1)}), s8[4194304]{0:T(1024)(128)(4,1)S(1)}, s32[]{:S(2)}) async-start(s8[4423680]{0:T(1024)(128)(4,1)} %bitcast.161), calls=%async_computation.2 | async-start | bytes 8388608
  197.1 6.8 %slice-start.1 = ((s8[4423680]{0:T(1024)(128)(4,1)}), s8[229376]{0:T(1024)(128)(4,1)S(1)}, s32[]{:S(2)}) async-start(s8[4423680]{0:T(1024)(128)(4,1)} %bitcast.161), calls=%async_computation.3 | async-start | bytes 458752
  205.9 20.8 %collective-permute-start.8 = (f32[1,16,3,5,2,256]{5,1,4,3,2,0:T(8,128)S(1)}, f32[1,16,3,5,2,256]{5,1,4,3,2,0:T(8,128)S(1)}, u32[]{:S(2)}, u32[]{:S(2)}) collective-permute-start(f32[1,16,3,5,2,256]{5,1,4,3,2,0:T(8,128)S(1)} %get-tuple-element.78), channel_id=1, source_target_pairs={{0,4},{4,8},{8,12},{12,16},{16,20},{20,24},{24,28},{1,5},{5,9},{9,... | collective-permute-start | bytes 1474568 | tf_op jit(solution)/shard_map/ppermute | solution.py:25
  208.3 21.1 %collective-permute-start.9 = (f32[1,16,3,5,2,256]{5,1,4,3,2,0:T(8,128)S(1)}, f32[1,16,3,5,2,256]{5,1,4,3,2,0:T(8,128)S(1)}, u32[]{:S(2)}, u32[]{:S(2)}) collective-permute-start(f32[1,16,3,5,2,256]{5,1,4,3,2,0:T(8,128)S(1)} %get-tuple-element.79), channel_id=1, source_target_pairs={{4,0},{8,4},{12,8},{16,12},{20,16},{24,20},{28,24},{5,1},{9,5},{13... | collective-permute-start | bytes 1474568 | tf_op jit(solution)/shard_map/ppermute | solution.py:27
  229.6 4.4 %collective-permute-start.10 = (f32[6,1,3,5,2,256]{5,1,4,3,2,0:T(1,128)S(1)}, f32[6,1,3,5,2,256]{5,1,4,3,2,0:T(1,128)S(1)}, u32[]{:S(2)}, u32[]{:S(2)}) collective-permute-start(f32[6,1,3,5,2,256]{5,1,4,3,2,0:T(1,128)S(1)} %get-tuple-element.72), channel_id=1, source_target_pairs={{0,1},{1,2},{2,3},{4,5},{5,6},{6,7},{8,9},{9,10},{10,11},{12,13},{... | collective-permute-start | bytes 552968 | tf_op jit(solution)/shard_map/ppermute | solution.py:25
  231.5 6.9 %collective-permute-start.11 = (f32[6,1,3,5,2,256]{5,1,4,3,2,0:T(1,128)S(1)}, f32[6,1,3,5,2,256]{5,1,4,3,2,0:T(1,128)S(1)}, u32[]{:S(2)}, u32[]{:S(2)}) collective-permute-start(f32[6,1,3,5,2,256]{5,1,4,3,2,0:T(1,128)S(1)} %get-tuple-element.73), channel_id=1, source_target_pairs={{1,0},{2,1},{3,2},{5,4},{6,5},{7,6},{9,8},{10,9},{11,10},{13,12},{... | collective-permute-start | bytes 552968 | tf_op jit(solution)/shard_map/ppermute | solution.py:27
  246.2 3.2 %copy-start.2 = (f32[6,18,3,5,2,256]{5,1,4,3,2,0:T(8,128)S(1)}, f32[6,18,3,5,2,256]{5,1,4,3,2,0:T(8,128)}, u32[]{:S(2)}) copy-start(f32[6,18,3,5,2,256]{5,1,4,3,2,0:T(8,128)} %scatter.14) | copy-start | bytes 9953284
  253.3 1.5 copy-start.3
  253.3 2.1 copy-start.4
  255.9 1.0 copy-start.6
  257.6 1.5 copy-start.5
  259.1 4.3 %copy-start.1 = (f32[32,32]{1,0:T(8,128)S(1)}, f32[32,32]{1,0:T(8,128)}, u32[]{:S(2)}) copy-start(f32[32,32]{1,0:T(8,128)} %param.19) | copy-start | bytes 12292
Sparse Core Ops, SparseCore 0:
  16.2 36.3 all-reduce.2
  56.1 76.3 all-reduce.4
